TPU v7x, 32 devices: a whole 2x2x4 slice. The times are simulated.
32 devices in a mesh: dp: 4 (over y, x), expert: 8 (over z, core).
Axes of the slice: x: 2, y: 2, z: 4, core: 2. Of those that a mesh axis runs over, the one named last changes fastest.
Arguments:
- tokens: bfloat16 [4096, 2048], P(('dp', 'expert')), may hold values from -6 to 6
- expert_ids: int32 [4096, 4], P(('dp', 'expert')), may hold values from 0 to 7, all different within a row; in each aligned block of 128 rows (0 to 127, 128 to 255, ...) at most 80 rows name the same one
- probs: float32 [4096, 4], P(('dp', 'expert')), may hold values from 0.2 to 1
- trade: int32 [4], replicated, may hold values from 0 to 1, as said below
- gate_weight: bfloat16 [8, 2048, 768], P('expert'), may hold values from -0.125 to 0.125
- up_weight: bfloat16 [8, 2048, 768], P('expert'), may hold values from -0.125 to 0.125
- down_weight: bfloat16 [8, 768, 2048], P('expert'), may hold values from -0.21875 to 0.21875
- out_grad: bfloat16 [4096, 2048], P(('dp', 'expert')), may hold values from -0.29882812 to 0.29882812
Outputs:
- combined: bfloat16 [4096, 2048], P(('dp', 'expert'))
- gate_grad: bfloat16 [8, 2048, 768], P('expert', 'dp')
- up_grad: bfloat16 [8, 2048, 768], P('expert', 'dp')
- down_grad: bfloat16 [8, 768, 2048], P('expert', None, 'dp')
Inputs may be any that keep to these rules, and one draw needn't show every extreme that they name: `trade`: index k below 4 pairs expert index k with k + 4; at least one pair trades and at least one does not. `expert_ids`: each row names 4 different experts. Within the 128 rows of one device no expert is named by more than 80 rows, a bound that some block reaches.
All inputs are finite; a program needn't handle non-finite values.
Results may differ from a plain program's by a relative error of at most 0.0095.
Values may be sent and summed in bfloat16 or wider, within the bound.
A program may use at most 128 MiB of HBM per device.

v0:
```python
import jax
import jax.numpy as jnp
from jax import lax
from jax.sharding import PartitionSpec as P


def sparse_local(tokens, expert_ids, probs, trade, gate_weight, up_weight, down_weight, out_grad):
    tok_count, model_width = tokens.shape
    top_count = expert_ids.shape[1]
    hidden_width = gate_weight.shape[2]
    experts = lax.axis_size("expert")
    capacity = 5 * tok_count * top_count // (4 * experts)
    halfway = experts // 2
    chosen = expert_ids.reshape(-1)
    numbers = jnp.arange(experts, dtype=jnp.int32)
    onehot = (chosen[:, None] == numbers[None, :]).astype(jnp.int32)
    earlier = jnp.cumsum(onehot, axis=0) - onehot
    slots = chosen * capacity + jnp.sum(earlier * onehot, axis=1)
    owners = jnp.where(trade[numbers % halfway] == 1, jnp.bitwise_xor(numbers, halfway), numbers)
    pair_tokens = jnp.arange(chosen.shape[0], dtype=jnp.int32) // top_count
    send_rows = (
        jnp.zeros((experts * capacity, model_width), jnp.bfloat16)
        .at[slots]
        .set(tokens[pair_tokens])
    )
    send_rows = send_rows.reshape(experts, capacity, model_width)
    out_pairs = (probs[:, :, None] * out_grad[:, None, :].astype(jnp.float32)).astype(jnp.bfloat16)
    send_grads = (
        jnp.zeros((experts * capacity, model_width), jnp.bfloat16)
        .at[slots]
        .set(out_pairs.reshape(-1, model_width))
    )
    send_grads = send_grads.reshape(experts, capacity, model_width)
    send_rows = send_rows[owners]
    send_grads = send_grads[owners]
    w_gate = gate_weight[0]
    w_up = up_weight[0]
    w_down = down_weight[0]
    arrived = lax.all_to_all(send_rows, "expert", split_axis=0, concat_axis=0, tiled=True)
    lead = arrived.shape[:2]
    flat_rows = arrived.reshape(-1, model_width)
    gate_act = jnp.dot(flat_rows, w_gate, preferred_element_type=jnp.float32)
    up_act = jnp.dot(flat_rows, w_up, preferred_element_type=jnp.float32)
    forward_hidden = (gate_act * jax.nn.sigmoid(gate_act) * up_act).astype(jnp.bfloat16)
    expert_out = jnp.dot(forward_hidden, w_down, preferred_element_type=jnp.float32).astype(
        jnp.bfloat16
    )
    arrived, expert_out, hidden, gate_act, up_act = (
        arrived,
        expert_out.reshape(lead + (model_width,)),
        forward_hidden.reshape(lead + (hidden_width,)),
        gate_act.reshape(lead + (hidden_width,)),
        up_act.reshape(lead + (hidden_width,)),
    )
    returned = lax.all_to_all(expert_out, "expert", split_axis=0, concat_axis=0, tiled=True)
    out_rows = lax.all_to_all(send_grads, "expert", split_axis=0, concat_axis=0, tiled=True)
    returned = returned[owners]
    picked = returned.reshape(-1, model_width)[slots].reshape(tok_count, top_count, model_width)
    combined = jnp.sum(probs[:, :, None] * picked.astype(jnp.float32), axis=1).astype(jnp.bfloat16)
    expert_rows = arrived.reshape(-1, model_width)
    out_rows = out_rows.reshape(-1, model_width)
    hidden = hidden.reshape(-1, hidden_width)
    gate_act = gate_act.reshape(-1, hidden_width)
    up_act = up_act.reshape(-1, hidden_width)
    hidden_grad = lax.dot_general(
        out_rows, w_down, (((1,), (1,)), ((), ())), preferred_element_type=jnp.float32
    )
    sigma = jax.nn.sigmoid(gate_act)
    gate_back = (hidden_grad * up_act * (sigma * (1.0 + gate_act * (1.0 - sigma)))).astype(
        jnp.bfloat16
    )
    up_back = (hidden_grad * (gate_act * sigma)).astype(jnp.bfloat16)
    both_back = jnp.concatenate([gate_back, up_back], axis=1)
    first = lax.dot_general(
        expert_rows, both_back, (((0,), (0,)), ((), ())), preferred_element_type=jnp.float32
    )
    second = lax.dot_general(
        out_rows, hidden, (((0,), (0,)), ((), ())), preferred_element_type=jnp.float32
    )
    summed = lax.psum_scatter(
        jnp.concatenate([first, second], axis=1).astype(jnp.bfloat16),
        "dp",
        scatter_dimension=0,
        tiled=True,
    )
    gate_part = summed[:, :hidden_width]
    up_part = summed[:, hidden_width : 2 * hidden_width]
    down_part = summed[:, 2 * hidden_width :].T
    return (combined, gate_part[None], up_part[None], down_part[None])


def dense_local(tokens, expert_ids, probs, trade, gate_weight, up_weight, down_weight, out_grad):
    hidden_width = gate_weight.shape[2]
    experts = lax.axis_size("expert")
    halfway = experts // 2
    me = lax.axis_index("expert")
    mine = jnp.where(trade[me % halfway] == 1, jnp.bitwise_xor(me, halfway), me)
    rows = lax.all_gather(tokens, "expert", axis=0, tiled=True)
    ids = lax.all_gather(expert_ids, "expert", axis=0, tiled=True)
    weights = lax.all_gather(probs, "expert", axis=0, tiled=True)
    grads = lax.all_gather(out_grad, "expert", axis=0, tiled=True)
    weight = jnp.sum(jnp.where(ids == mine, weights, 0.0), axis=1, keepdims=True)
    w_gate = gate_weight[0]
    w_up = up_weight[0]
    w_down = down_weight[0]
    gate_act = jnp.dot(rows, w_gate, preferred_element_type=jnp.float32)
    up_act = jnp.dot(rows, w_up, preferred_element_type=jnp.float32)
    sigma = jax.nn.sigmoid(gate_act)
    hidden = (gate_act * sigma * up_act).astype(jnp.bfloat16)
    expert_out = jnp.dot(hidden, w_down, preferred_element_type=jnp.float32)
    part = (weight * expert_out).astype(jnp.bfloat16)
    out_rows = (weight * grads.astype(jnp.float32)).astype(jnp.bfloat16)
    hidden_grad = lax.dot_general(
        out_rows, w_down, (((1,), (1,)), ((), ())), preferred_element_type=jnp.float32
    )
    gate_back = (hidden_grad * up_act * (sigma * (1.0 + gate_act * (1.0 - sigma)))).astype(
        jnp.bfloat16
    )
    up_back = (hidden_grad * (gate_act * sigma)).astype(jnp.bfloat16)
    both_back = jnp.concatenate([gate_back, up_back], axis=1)
    first = lax.dot_general(
        rows, both_back, (((0,), (0,)), ((), ())), preferred_element_type=jnp.float32
    )
    second = lax.dot_general(
        out_rows, hidden, (((0,), (0,)), ((), ())), preferred_element_type=jnp.float32
    )
    summed = lax.psum_scatter(
        jnp.concatenate([first, second], axis=1).astype(jnp.bfloat16),
        "dp",
        scatter_dimension=0,
        tiled=True,
    )
    combined = lax.psum_scatter(part, "expert", scatter_dimension=0, tiled=True)
    gate_part = summed[:, :hidden_width]
    up_part = summed[:, hidden_width : 2 * hidden_width]
    down_part = summed[:, 2 * hidden_width :].T
    return (combined, gate_part[None], up_part[None], down_part[None])


def local(tokens, expert_ids, *rest):
    capacity = 5 * tokens.shape[0] * expert_ids.shape[1] // (4 * lax.axis_size("expert"))
    if tokens.shape[0] <= 2 * capacity:
        return dense_local(tokens, expert_ids, *rest)
    return sparse_local(tokens, expert_ids, *rest)


def solution(mesh):
    return jax.shard_map(
        local,
        mesh=mesh,
        in_specs=(
            P(("dp", "expert"), None),
            P(("dp", "expert"), None),
            P(("dp", "expert"), None),
            P(),
            P("expert", None, None),
            P("expert", None, None),
            P("expert", None, None),
            P(("dp", "expert"), None),
        ),
        out_specs=(
            P(("dp", "expert"), None),
            P("expert", "dp", None),
            P("expert", "dp", None),
            P("expert", None, "dp"),
        ),
        check_vma=False,
    )
```

profile of v0, /device:TPU:0, one launch (start us, length us, event | category | flops | bytes accessed | tf_op | source)
XLA Modules:
  0.0 297.5 jit_solution(16371395438921488804)
XLA Ops:
  7.2 0.0 copy-start
  7.2 0.0 all-gather.3.cloned.1.call-start
  7.2 0.7 all-gather.3.cloned.1.call-update
  7.9 0.0 all-gather.5.cloned.1.call-start
  8.0 0.7 all-gather.5.cloned.1.call-update
  8.7 0.0 reduce-scatter.5.cloned.1.call-start
  8.7 1.2 dynamic_slice.3
  10.6 14.7 %all_gather.13 = f32[1024,4]{0,1:T(4,128)S(1)} all-gather(f32[128,4]{0,1:T(4,128)} %param.10), channel_id=1, replica_groups=mesh['dp'=4,'expert'=8] {'expert'}, dimensions={0}, use_global_device_ids=true | all-gather | bytes 18432 | tf_op jit(solution)/shard_map/all_gather | solution.py:100
  25.3 13.3 %all_gather.12 = s32[1024,4]{0,1:T(4,128)S(1)} all-gather(s32[128,4]{0,1:T(4,128)} %param.9), channel_id=1, replica_groups=mesh['dp'=4,'expert'=8] {'expert'}, dimensions={0}, use_global_device_ids=true | all-gather | bytes 18432 | tf_op jit(solution)/shard_map/all_gather | solution.py:99
  38.7 20.7 %all-gather.3.cloned.1.call-done = bf16[1024,2048]{1,0:T(8,128)(2,1)} async-done(((bf16[128,2048]{1,0:T(8,128)(2,1)}), bf16[1024,2048]{1,0:T(8,128)(2,1)}) %all-gather.3.cloned.1.call-update) | async-done | bytes 4194320 | tf_op jit(solution)/shard_map/all_gather | solution.py:98
  59.4 8.3 %fusion.7 = f32[1024,768]{0,1:T(8,128)} fusion(bf16[1024,2048]{1,0:T(8,128)(2,1)} %all-gather.3.cloned.1.call-done, bf16[1,2048,768]{2,1,0:T(8,128)(2,1)} %param.13), kind=kOutput, calls=%fused_computation.12 | convolution fusion | flops 3221225472 | bytes 10485760 | tf_op jit(solution)/shard_map/dot_general | solution.py:107
  67.7 38.9 %all-gather.5.cloned.1.call-done = bf16[1024,2048]{1,0:T(8,128)(2,1)} async-done(((bf16[128,2048]{1,0:T(8,128)(2,1)}), bf16[1024,2048]{1,0:T(8,128)(2,1)}) %all-gather.5.cloned.1.call-update) | async-done | bytes 4194320 | tf_op jit(solution)/shard_map/all_gather | solution.py:101
  106.6 0.0 copy-done
  106.6 0.0 copy-start.1
  106.7 0.0 copy-start.3
  106.7 5.8 %fusion.4 = f32[1024,768]{0,1:T(8,128)S(1)} fusion(bf16[1,768,2048]{2,1,0:T(8,128)(2,1)S(1)} %copy-done, bf16[1024,2048]{1,0:T(8,128)(2,1)} %all-gather.5.cloned.1.call-done, f32[1024]{0:T(1024)S(1)} %select_reduce_fusion), kind=kOutput, calls=%fused_computation.9 | convolution fusion | flops 3227516928 | bytes 10489856 | tf_op jit(solution)/shard_map/dot_general | solution.py:113
  112.5 0.0 copy-done.1
  112.5 0.0 copy-done.3
  112.5 0.0 copy-start.2
  112.5 7.9 %multiply_convert_fusion.3 = (bf16[1024,768]{0,1:T(8,128)(2,1)}, bf16[1024,768]{0,1:T(8,128)(2,1)}, bf16[1024,768]{0,1:T(8,128)(2,1)S(1)}) fusion(f32[1024,768]{0,1:T(8,128)S(1)} %fusion.4, f32[1024,768]{0,1:T(8,128)} %fusion.7, bf16[1024,2048]{1,0:T(8,128)(2,1)S(1)} %copy-done.1, bf16[1,2048,768]{2,1,0:T(8,128)(2,1)S(1)} %copy-done.3), kind=kOutput, calls=%fused_computation.17 | convolution fusion | flops 3233021952 | bytes 18350080 | tf_op jit(solution)/shard_map/dot_general | solution.py:106
  120.4 0.0 copy-start.4
  120.4 0.0 copy-done.2
  120.4 0.0 copy-start.5
  120.4 0.0 copy-start.6
  120.4 3.9 %convolution_convert_fusion.1 = bf16[2048,768]{0,1:T(8,128)(2,1)S(1)} fusion(bf16[1024,768]{0,1:T(8,128)(2,1)S(1)} %get-tuple-element.10, bf16[1024,2048]{1,0:T(8,128)(2,1)S(1)} %copy-done.2, f32[1024]{0:T(1024)S(1)} %select_reduce_fusion), kind=kOutput, calls=%fused_computation.5 | convolution fusion | flops 3229089792 | bytes 8916992 | tf_op jit(solution)/shard_map/dot_general | solution.py:124
  124.3 0.0 copy-done.4
  124.3 0.0 copy-done.5
  124.3 0.0 copy-done.6
  124.3 8.5 %fusion = bf16[2048,1536]{0,1:T(8,128)(2,1)S(1)} fusion(bf16[1024,2048]{1,0:T(8,128)(2,1)S(1)} %copy-done.1, bf16[1024,768]{0,1:T(8,128)(2,1)S(1)} %copy-done.6, bf16[1024,768]{0,1:T(8,128)(2,1)S(1)} %copy-done.5), kind=kOutput, calls=%fused_computation.4 | convolution fusion | flops 6451888128 | bytes 13631488 | tf_op jit(solution)/shard_map/dot_general | solution.py:121
  132.8 11.6 %pad_maximum_fusion = bf16[2048,2304]{0,1:T(8,128)(2,1)} fusion(bf16[2048,768]{0,1:T(8,128)(2,1)S(1)} %convolution_convert_fusion.1, bf16[2048,1536]{0,1:T(8,128)(2,1)S(1)} %fusion), kind=kLoop, calls=%fused_computation | loop fusion | flops 18874368 | bytes 18874368 | tf_op jit(solution)/shard_map/concatenate | solution.py:128
  144.4 0.0 reduce-scatter.5.cloned.1.call-update
  144.5 0.0 reduce-scatter.3.cloned.1.call-start
  144.5 6.7 %multiply_convert_fusion.1 = bf16[1024,2048]{1,0:T(8,128)(2,1)} fusion(bf16[1024,768]{0,1:T(8,128)(2,1)} %copy-done.4, f32[1024]{0:T(1024)S(1)} %select_reduce_fusion, bf16[1,768,2048]{2,1,0:T(8,128)(2,1)S(1)} %copy-done), kind=kOutput, calls=%fused_computation.2 | convolution fusion | flops 3225419776 | bytes 8916992 | tf_op jit(solution)/shard_map/dot_general | solution.py:110
  151.2 0.0 reduce-scatter.3.cloned.1.call-update
  151.3 87.0 %reduce-scatter.5.cloned.1.call-done = bf16[512,2304]{0,1:T(8,128)(2,1)} async-done(((bf16[2048,2304]{0,1:T(8,128)(2,1)}), bf16[512,2304]{0,1:T(8,128)(2,1)}) %reduce-scatter.5.cloned.1.call-update) | async-done | bytes 2359312 | tf_op jit(solution)/shard_map/reduce_scatter | solution.py:127
  238.3 3.1 %slice_bitcast_fusion = (bf16[1,768,512]{2,1,0:T(8,128)(2,1)}, bf16[1,512,768]{1,2,0:T(8,128)(2,1)}, bf16[1,512,768]{1,2,0:T(8,128)(2,1)}) fusion(bf16[512,2304]{0,1:T(8,128)(2,1)} %reduce-scatter.5.cloned.1.call-done), kind=kLoop, calls=%fused_computation.21 | loop fusion | bytes 4718592 | tf_op jit(solution)/shard_map/broadcast_in_dim | solution.py:137
  241.4 2.3 copy.12
  243.7 2.3 copy.13
  245.9 45.0 %reduce-scatter.3.cloned.1.call-done = bf16[128,2048]{1,0:T(8,128)(2,1)} async-done(((bf16[1024,2048]{1,0:T(8,128)(2,1)}), bf16[128,2048]{1,0:T(8,128)(2,1)}) %reduce-scatter.3.cloned.1.call-update) | async-done | bytes 524304 | tf_op jit(solution)/shard_map/reduce_scatter | solution.py:133
  (1 shorter events, 0.0 us)
Async XLA Ops:
  7.2 99.5 %copy-start = (bf16[1,768,2048]{2,1,0:T(8,128)(2,1)S(1)}, bf16[1,768,2048]{2,1,0:T(8,128)(2,1)}, u32[]{:S(2)}) copy-start(bf16[1,768,2048]{2,1,0:T(8,128)(2,1)} %param.14) | copy-start | bytes 9437188
  7.2 52.2 %all-gather.3.cloned.1.call-start = ((), (), s32[]{:S(2)}) async-start(), calls=%async_computation.2 | async-start | bytes 4718592 | tf_op jit(solution)/shard_map/all_gather | solution.py:98
  7.9 98.7 %all-gather.5.cloned.1.call-start = ((), (), s32[]{:S(2)}) async-start(), calls=%async_computation.4 | async-start | bytes 4718592 | tf_op jit(solution)/shard_map/all_gather | solution.py:101
  8.7 229.7 %reduce-scatter.5.cloned.1.call-start = ((), (), s32[]{:S(2)}) async-start(), calls=%async_computation.5 | async-start | bytes 11796480 | tf_op jit(solution)/shard_map/reduce_scatter | solution.py:127
  106.6 5.8 %copy-start.1 = (bf16[1024,2048]{1,0:T(8,128)(2,1)S(1)}, bf16[1024,2048]{1,0:T(8,128)(2,1)}, u32[]{:S(2)}) copy-start(bf16[1024,2048]{1,0:T(8,128)(2,1)} %all-gather.3.cloned.1.call-done) | copy-start | bytes 12582916
  106.7 5.9 %copy-start.3 = (bf16[1,2048,768]{2,1,0:T(8,128)(2,1)S(1)}, bf16[1,2048,768]{2,1,0:T(8,128)(2,1)}, u32[]{:S(2)}) copy-start(bf16[1,2048,768]{2,1,0:T(8,128)(2,1)} %param.12) | copy-start | bytes 9437188
  112.5 7.9 %copy-start.2 = (bf16[1024,2048]{1,0:T(8,128)(2,1)S(1)}, bf16[1024,2048]{1,0:T(8,128)(2,1)}, u32[]{:S(2)}) copy-start(bf16[1024,2048]{1,0:T(8,128)(2,1)} %all-gather.5.cloned.1.call-done) | copy-start | bytes 12582916
  120.4 3.9 %copy-start.4 = (bf16[1024,768]{0,1:T(8,128)(2,1)}, bf16[1024,768]{0,1:T(8,128)(2,1)S(1)}, u32[]{:S(2)}) copy-start(bf16[1024,768]{0,1:T(8,128)(2,1)S(1)} %get-tuple-element.10) | copy-start | bytes 4718596
  120.4 3.9 %copy-start.5 = (bf16[1024,768]{0,1:T(8,128)(2,1)S(1)}, bf16[1024,768]{0,1:T(8,128)(2,1)}, u32[]{:S(2)}) copy-start(bf16[1024,768]{0,1:T(8,128)(2,1)} %get-tuple-element.8) | copy-start | bytes 4718596
  120.4 3.9 %copy-start.6 = (bf16[1024,768]{0,1:T(8,128)(2,1)S(1)}, bf16[1024,768]{0,1:T(8,128)(2,1)}, u32[]{:S(2)}) copy-start(bf16[1024,768]{0,1:T(8,128)(2,1)} %get-tuple-element.9) | copy-start | bytes 4718596
  144.5 146.5 %reduce-scatter.3.cloned.1.call-start = ((), (), s32[]{:S(2)}) async-start(), calls=%async_computation.3 | async-start | bytes 4718592 | tf_op jit(solution)/shard_map/reduce_scatter | solution.py:133
Sparse Core Ops, SparseCore 0:
  9.6 49.7 all-gather.2
  61.0 45.6 all-gather.4
  144.6 93.6 reduce-scatter.4
  241.0 49.8 reduce-scatter.2
where the time goes:
time: 298 us
  waiting for transfers between devices  193 us (65%)
  matrix products  41.2 us (14%)
  blocking collectives  28 us (9%)
  between operations  14.5 us (5%)
  other arithmetic  11.6 us (4%)
  local copies, waits for them, and re-layouts  8.9 us (3%)
    reduce_scatter x1, waiting for transfers between devices, dense_local(): lax.psum_scatter(jnp.concatenate([first, second], axis=1).astype(jnp.bflo...  87 us
    reduce_scatter x1, waiting for transfers between devices, dense_local(): combined = lax.psum_scatter(part, 'expert', scatter_dimension=0, tiled=True)  45 us
    all_gather x1, waiting for transfers between devices, dense_local(): grads = lax.all_gather(out_grad, 'expert', axis=0, tiled=True)  38.9 us
    all_gather x1, waiting for transfers between devices, dense_local(): rows = lax.all_gather(tokens, 'expert', axis=0, tiled=True)  20.7 us
    all_gather x1, blocking collectives, dense_local(): weights = lax.all_gather(probs, 'expert', axis=0, tiled=True)  14.7 us
    all_gather x1, blocking collectives, dense_local(): ids = lax.all_gather(expert_ids, 'expert', axis=0, tiled=True)  13.3 us
    concatenate x1, other arithmetic, dense_local(): jnp.concatenate([first, second], axis=1).astype(jnp.bfloat16)  11.6 us
    dot_general x1, matrix products, dense_local(): lax.dot_general(rows, both_back, (((0,), (0,)), ((), ())), preferred_elem...  8.5 us
  transfers between devices with their start and end apart: 4, of which 4 were waited for; matrix products, arithmetic and copies ran while one was open for 8% of the time, Pallas kernels for 0%

commit v1 on v0

--- a/solution.py
+++ b/solution.py
@@ -98,7 +98,9 @@
     rows = lax.all_gather(tokens, "expert", axis=0, tiled=True)
     ids = lax.all_gather(expert_ids, "expert", axis=0, tiled=True)
     weights = lax.all_gather(probs, "expert", axis=0, tiled=True)
-    grads = lax.all_gather(out_grad, "expert", axis=0, tiled=True)
+    grads = jnp.concatenate(
+        lax.all_to_all(jnp.stack([out_grad] * lax.axis_size("expert")), "expert", 0, 0), axis=0
+    )
     weight = jnp.sum(jnp.where(ids == mine, weights, 0.0), axis=1, keepdims=True)
     w_gate = gate_weight[0]
     w_up = up_weight[0]

time: 298 us -> 371 us (1.24)
  blocking collectives: 28 us -> 144 us
  waiting for transfers between devices: 193 us -> 133 us
  other arithmetic: 11.6 us -> 19.4 us
  starting transfers between devices: 0.16 us -> 6.6 us
    all_gather x1, blocking collectives: 14.7 us -> 132 us  [dense_local(): weights = lax.all_gather(probs, 'expert', axis=0, tiled=True)]
    all_gather x1 -> x0, waiting for transfers between devices: 38.9 us -> none  [dense_local(): grads = lax.all_gather(out_grad, 'expert', axis=0, tiled=True)]
    all_gather x1, waiting for transfers between devices: 20.7 us -> 0.01 us  [dense_local(): rows = lax.all_gather(tokens, 'expert', axis=0, tiled=True)]
    convert_element_type x0 -> x2, other arithmetic: none -> 7.81 us  [dense_local(): out_rows = (weight * grads.astype(jnp.float32)).astype(jnp.bfloat16)]
    all_to_all x0 -> x1, starting transfers between devices: none -> 6.49 us  [dense_local(): lax.all_to_all(jnp.stack([out_grad] * lax.axis_size('expert')), 'expert',...]
  transfers between devices with their start and end apart: 4 -> 4, of which waited for: 4 -> 2; matrix products, arithmetic and copies ran while one was open for 8% -> 7% of each run, Pallas kernels for 0% -> 0%
where the time goes in v1:
time: 371 us; the launch traced here: 370 us
  blocking collectives  144 us (39%)
  waiting for transfers between devices  133 us (36%)
  matrix products  40.4 us (11%)
  other arithmetic  19.4 us (5%)
  between operations  14.6 us (4%)
  local copies, waits for them, and re-layouts  11.9 us (3%)
  starting transfers between devices  6.6 us (2%)
    all_gather x1, blocking collectives, dense_local(): weights = lax.all_gather(probs, 'expert', axis=0, tiled=True)  132 us
    reduce_scatter x1, waiting for transfers between devices, dense_local(): lax.psum_scatter(jnp.concatenate([first, second], axis=1).astype(jnp.bflo...  87.1 us
    reduce_scatter x1, waiting for transfers between devices, dense_local(): combined = lax.psum_scatter(part, 'expert', scatter_dimension=0, tiled=True)  45.2 us
    all_gather x1, blocking collectives, dense_local(): ids = lax.all_gather(expert_ids, 'expert', axis=0, tiled=True)  12.8 us
    concatenate x1, other arithmetic, dense_local(): jnp.concatenate([first, second], axis=1).astype(jnp.bfloat16)  11.6 us
    dot_general x1, matrix products, dense_local(): lax.dot_general(rows, both_back, (((0,), (0,)), ((), ())), preferred_elem...  8.5 us
    dot_general x1, matrix products, dense_local(): up_act = jnp.dot(rows, w_up, preferred_element_type=jnp.float32)  8.48 us
    dot_general x1, matrix products, dense_local(): gate_act = jnp.dot(rows, w_gate, preferred_element_type=jnp.float32)  8.06 us
  transfers between devices with their start and end apart: 4, of which 2 were waited for; matrix products, arithmetic and copies ran while one was open for 7% of the time, Pallas kernels for 0%

profile of v1, /device:TPU:0, one launch (start us, length us, event | category | flops | bytes accessed | tf_op | source)
XLA Modules:
  0.0 370.4 jit_solution(13234150713163792436)
XLA Ops:
  7.2 0.0 copy-start
  7.2 3.7 stack.2
  10.9 0.0 copy-start.6
  10.9 0.0 copy-start.2
  10.9 0.0 copy-start.3
  10.9 6.5 %all-to-all-start = ((bf16[8,128,2048]{2,1,0:T(8,128)(2,1)}), bf16[8,128,2048]{2,1,0:T(8,128)(2,1)}, u32[]{:S(2)}, u32[]{:S(2)}) async-start(bf16[8,128,2048]{2,1,0:T(8,128)(2,1)} %stack.2), calls=%async_computation.1 | async-start | bytes 8388608 | tf_op jit(solution)/shard_map/all_to_all | solution.py:102
  17.3 0.0 all-gather.2.cloned.1.call-start
  17.4 0.7 all-gather.2.cloned.1.call-update
  18.1 0.0 reduce-scatter.5.cloned.1.call-start
  18.1 0.0 copy-done.6
  18.2 0.6 dynamic_slice.3
  19.4 0.0 copy-done.2
  19.4 131.7 %all_gather.10 = f32[1024,4]{0,1:T(4,128)S(1)} all-gather(f32[128,4]{0,1:T(4,128)S(1)} %copy-done.2), channel_id=1, replica_groups=mesh['dp'=4,'expert'=8] {'expert'}, dimensions={0}, use_global_device_ids=true | all-gather | bytes 18432 | tf_op jit(solution)/shard_map/all_gather | solution.py:100
  151.1 0.0 copy-done.3
  151.1 12.8 %all_gather.9 = s32[1024,4]{0,1:T(4,128)S(1)} all-gather(s32[128,4]{0,1:T(4,128)S(1)} %copy-done.3), channel_id=1, replica_groups=mesh['dp'=4,'expert'=8] {'expert'}, dimensions={0}, use_global_device_ids=true | all-gather | bytes 18432 | tf_op jit(solution)/shard_map/all_gather | solution.py:99
  163.9 0.0 all-to-all-done
  163.9 4.9 %fusion = bf16[1024,2048]{1,0:T(8,128)(2,1)} fusion(f32[1024]{0:T(1024)S(1)} %select_reduce_fusion, bf16[8,128,2048]{2,1,0:T(8,128)(2,1)} %all-to-all-done), kind=kLoop, calls=%fused_computation.2 | loop fusion | flops 6291456 | bytes 8392704 | tf_op jit(solution)/shard_map/convert_element_type | solution.py:114
  168.8 2.9 multiply_convert_fusion
  171.7 0.0 copy-done
  171.7 5.2 %fusion.5 = f32[1024,768]{0,1:T(8,128)} fusion(bf16[1024,2048]{1,0:T(8,128)(2,1)S(1)} %bitcast.37, bf16[1,768,2048]{2,1,0:T(8,128)(2,1)S(1)} %copy-done), kind=kOutput, calls=%fused_computation.11 | convolution fusion | flops 3221225472 | bytes 10485760 | tf_op jit(solution)/shard_map/dot_general | solution.py:115
  176.9 0.0 all-gather.2.cloned.1.call-done
  176.9 0.0 copy-start.4
  176.9 0.0 copy-start.5
  176.9 0.0 copy-start.7
  176.9 8.5 %fusion.8 = f32[1024,768]{0,1:T(8,128)} fusion(bf16[1024,2048]{1,0:T(8,128)(2,1)} %all-gather.2.cloned.1.call-done, bf16[1,2048,768]{2,1,0:T(8,128)(2,1)} %param.13), kind=kOutput, calls=%fused_computation.14 | convolution fusion | flops 3221225472 | bytes 10485760 | tf_op jit(solution)/shard_map/dot_general | solution.py:109
  185.4 0.0 copy-done.4
  185.4 0.0 copy-done.5
  185.4 0.0 copy-done.7
  185.4 0.0 copy-start.1
  185.4 8.1 %multiply_convert_fusion.3 = (bf16[1024,768]{0,1:T(8,128)(2,1)}, bf16[1024,768]{0,1:T(8,128)(2,1)}, bf16[1024,768]{0,1:T(8,128)(2,1)S(1)}) fusion(f32[1024,768]{0,1:T(8,128)S(1)} %copy-done.7, f32[1024,768]{0,1:T(8,128)} %fusion.8, bf16[1024,2048]{1,0:T(8,128)(2,1)S(1)} %copy-done.4, bf16[1,2048,768]{2,1,0:T(8,128)(2,1)S(1)} %copy-done.5), kind=kOutput, calls=%fused_computation.19 | convolution fusion | flops 3233021952 | bytes 18350080 | tf_op jit(solution)/shard_map/dot_general | solution.py:108
  193.5 0.0 copy-done.1
  193.5 0.0 copy-start.9
  193.5 0.0 copy-start.10
  193.5 3.6 convolution_convert_fusion.1
  197.2 0.0 copy-done.8
  197.2 0.0 copy-done.9
  197.2 0.0 copy-done.10
  197.2 8.5 %fusion.1 = bf16[2048,1536]{0,1:T(8,128)(2,1)S(1)} fusion(bf16[1024,2048]{1,0:T(8,128)(2,1)S(1)} %copy-done.4, bf16[1024,768]{0,1:T(8,128)(2,1)S(1)} %copy-done.10, bf16[1024,768]{0,1:T(8,128)(2,1)S(1)} %copy-done.9), kind=kOutput, calls=%fused_computation.6 | convolution fusion | flops 6451888128 | bytes 13631488 | tf_op jit(solution)/shard_map/dot_general | solution.py:123
  205.7 11.6 %pad_maximum_fusion = bf16[2048,2304]{0,1:T(8,128)(2,1)} fusion(bf16[2048,768]{0,1:T(8,128)(2,1)S(1)} %convolution_convert_fusion.1, bf16[2048,1536]{0,1:T(8,128)(2,1)S(1)} %fusion.1), kind=kLoop, calls=%fused_computation | loop fusion | flops 18874368 | bytes 18874368 | tf_op jit(solution)/shard_map/concatenate | solution.py:130
  217.3 0.0 reduce-scatter.5.cloned.1.call-update
  217.3 0.0 reduce-scatter.3.cloned.1.call-start
  217.4 6.5 %multiply_convert_fusion.1 = bf16[1024,2048]{1,0:T(8,128)(2,1)} fusion(bf16[1024,768]{0,1:T(8,128)(2,1)} %copy-done.8, f32[1024]{0:T(1024)S(1)} %select_reduce_fusion, bf16[1,768,2048]{2,1,0:T(8,128)(2,1)S(1)} %copy-done), kind=kOutput, calls=%fused_computation.4 | convolution fusion | flops 3225419776 | bytes 8916992 | tf_op jit(solution)/shard_map/dot_general | solution.py:112
  223.9 0.0 reduce-scatter.3.cloned.1.call-update
  223.9 87.1 %reduce-scatter.5.cloned.1.call-done = bf16[512,2304]{0,1:T(8,128)(2,1)} async-done(((bf16[2048,2304]{0,1:T(8,128)(2,1)}), bf16[512,2304]{0,1:T(8,128)(2,1)}) %reduce-scatter.5.cloned.1.call-update) | async-done | bytes 2359312 | tf_op jit(solution)/shard_map/reduce_scatter | solution.py:129
  311.0 3.1 slice_bitcast_fusion
  314.1 2.3 copy.12
  316.3 2.3 copy.13
  318.6 45.2 %reduce-scatter.3.cloned.1.call-done = bf16[128,2048]{1,0:T(8,128)(2,1)} async-done(((bf16[1024,2048]{1,0:T(8,128)(2,1)}), bf16[128,2048]{1,0:T(8,128)(2,1)}) %reduce-scatter.3.cloned.1.call-update) | async-done | bytes 524304 | tf_op jit(solution)/shard_map/reduce_scatter | solution.py:135
  (2 shorter events, 0.0 us)
Async XLA Ops:
  7.2 164.6 %copy-start = (bf16[1,768,2048]{2,1,0:T(8,128)(2,1)S(1)}, bf16[1,768,2048]{2,1,0:T(8,128)(2,1)}, u32[]{:S(2)}) copy-start(bf16[1,768,2048]{2,1,0:T(8,128)(2,1)} %param.14) | copy-start | bytes 9437188
  10.9 7.3 %copy-start.6 = (s32[4]{0:T(128)S(1)}, s32[4]{0:T(128)}, u32[]{:S(2)}) copy-start(s32[4]{0:T(128)} %param.11) | copy-start | bytes 52
  10.9 8.5 %copy-start.2 = (f32[128,4]{0,1:T(4,128)S(1)}, f32[128,4]{0,1:T(4,128)}, u32[]{:S(2)}) copy-start(f32[128,4]{0,1:T(4,128)} %param.10) | copy-start | bytes 6148
  10.9 140.3 %copy-start.3 = (s32[128,4]{0,1:T(4,128)S(1)}, s32[128,4]{0,1:T(4,128)}, u32[]{:S(2)}) copy-start(s32[128,4]{0,1:T(4,128)} %param.9) | copy-start | bytes 6148
  10.9 153.0 %all-to-all-start = ((bf16[8,128,2048]{2,1,0:T(8,128)(2,1)}), bf16[8,128,2048]{2,1,0:T(8,128)(2,1)}, u32[]{:S(2)}, u32[]{:S(2)}) async-start(bf16[8,128,2048]{2,1,0:T(8,128)(2,1)} %stack.2), calls=%async_computation.1 | async-start | bytes 8388608 | tf_op jit(solution)/shard_map/all_to_all | solution.py:102
  17.3 159.6 %all-gather.2.cloned.1.call-start = ((), (), s32[]{:S(2)}) async-start(), calls=%async_computation.3 | async-start | bytes 4718592 | tf_op jit(solution)/shard_map/all_gather | solution.py:98
  18.1 292.9 %reduce-scatter.5.cloned.1.call-start = ((), (), s32[]{:S(2)}) async-start(), calls=%async_computation.5 | async-start | bytes 11796480 | tf_op jit(solution)/shard_map/reduce_scatter | solution.py:129
  176.9 8.5 %copy-start.4 = (bf16[1024,2048]{1,0:T(8,128)(2,1)S(1)}, bf16[1024,2048]{1,0:T(8,128)(2,1)}, u32[]{:S(2)}) copy-start(bf16[1024,2048]{1,0:T(8,128)(2,1)} %all-gather.2.cloned.1.call-done) | copy-start | bytes 12582916
  176.9 8.5 %copy-start.5 = (bf16[1,2048,768]{2,1,0:T(8,128)(2,1)S(1)}, bf16[1,2048,768]{2,1,0:T(8,128)(2,1)}, u32[]{:S(2)}) copy-start(bf16[1,2048,768]{2,1,0:T(8,128)(2,1)} %param.12) | copy-start | bytes 9437188
  176.9 8.5 %copy-start.7 = (f32[1024,768]{0,1:T(8,128)S(1)}, f32[1024,768]{0,1:T(8,128)}, u32[]{:S(2)}) copy-start(f32[1024,768]{0,1:T(8,128)} %fusion.5) | copy-start | bytes 9437188
  185.4 8.1 %copy-start.1 = (bf16[1024,2048]{1,0:T(8,128)(2,1)S(1)}, bf16[1024,2048]{1,0:T(8,128)(2,1)}, u32[]{:S(2)}) copy-start(bf16[1024,2048]{1,0:T(8,128)(2,1)} %fusion) | copy-start | bytes 12582916
  193.5 3.7 copy-start.8
  193.5 3.7 copy-start.9
  193.5 3.7 copy-start.10
  217.3 146.5 %reduce-scatter.3.cloned.1.call-start = ((), (), s32[]{:S(2)}) async-start(), calls=%async_computation.4 | async-start | bytes 4718592 | tf_op jit(solution)/shard_map/reduce_scatter | solution.py:135
Sparse Core Ops, SparseCore 0:
  19.8 81.5 all-gather.1
  217.5 93.4 reduce-scatter.4
  313.9 49.8 reduce-scatter.2
